TPU v7x, 512 devices: a whole 4x8x8 slice. The times are simulated.
512 devices in a mesh: face: 16 (over x, z_hi, core), patch: 32 (over z_lo, y).
Axes of the slice: x: 4, y: 8, z: 8 (z_hi: 2, z_lo: 4; z = z_hi * 4 + z_lo), core: 2. Of those that a mesh axis runs over, the one named last changes fastest.
Arguments:
- dust_map: float32 [128, 32768], P('face', 'patch'), may hold values from -12 to 12
- seam_flags: int32 [16, 32, 4], P('face', 'patch'), may hold values from 0 to 1
- block_weights: int32 [128, 4096], P('face', 'patch'), may hold values from 1 to 4
Outputs:
- energy_field: float32 [128, 32768], P('face', 'patch')
- face_moments: float32 [16, 3, 128], P('face')
- sky_moments: float32 [3, 128], replicated
All inputs are finite; a program needn't handle non-finite values.
Results may differ from a plain program's by a relative error of at most 0.0003.
Values sent between devices are 32-bit elements; how exact they have to be, the bound alone decides.
No kernel may reach another device: no remote copies, remote signals or barrier semaphores. Data moves between devices by JAX's collectives and lax.ppermute only.
A program may use at most 64 MiB of HBM per device.

v0:
```python
import math

import jax
import jax.numpy as jnp
import numpy as np
from jax import lax
from jax.experimental import pallas as pl
from jax.experimental.pallas import tpu as pltpu
from jax.sharding import Mesh
from jax.sharding import PartitionSpec as P

EPS = 1e-06
PAIRS = ((0, 1), (0, 2), (1, 2))
FACE = ("x", "zh", "core")
PATCH = ("zl", "y")
FLAG_LANE = 32


def filter_features():
    rows = np.repeat(np.array([-1.0, 0.0, 1.0]), 3)
    cols = np.tile(np.array([-1.0, 0.0, 1.0]), 3)
    env = np.exp(-(rows**2 + cols**2) / 1.28)
    at = {(int(a), int(b)): i for i, (a, b) in enumerate(zip(rows, cols))}
    picks = [at[0, 1], at[1, 0], at[1, 1], at[1, -1]]
    even, odd = [], []
    for t in range(8):
        h = math.pi * t / 8.0
        ph = 2.2 * (rows * math.cos(h) + cols * math.sin(h))
        c = np.cos(ph) - np.sum(env * np.cos(ph)) / np.sum(env)
        s = np.sin(ph) - np.sum(env * np.sin(ph)) / np.sum(env)
        norm = np.sqrt(np.sum(env**2 * (c**2 + s**2)))
        for src, dst in ((env * c / norm, even), (env * s / norm, odd)):
            v = src[picks]
            dst.append([v[0], v[1], (v[2] + v[3]) / 2, (v[2] - v[3]) / 2])
    out = np.array([even, odd])
    out[np.abs(out) < 1e-12] = 0.0
    return out


TABLE = filter_features()


def features(top, mid, bot, left, right):
    tl, tr = left(top), right(top)
    ml, mr = left(mid), right(mid)
    bl, br = left(bot), right(bot)
    top, mid, bot = (v[len(v) // 2] if isinstance(v, tuple) else v for v in (top, mid, bot))
    two = mid + mid
    s1, s2 = br + tl, bl + tr
    d1, d2 = br - tl, bl - tr
    return (
        ml + mr - two,
        top + bot - two,
        s1 + s2 - (two + two),
        s1 - s2,
        mr - ml,
        bot - top,
        d1 + d2,
        d1 - d2,
    )


def combos(ft):
    e01, e10, p, q, o01, o10, po, qo = ft

    def lin(pairs):
        total = None
        for c, v in pairs:
            if c == 0.0:
                continue
            term = float(c) * v
            total = term if total is None else total + term
        return total

    re, im = [None] * 8, [None] * 8
    for t in (0, 4):
        ce, co = TABLE[0, t], TABLE[1, t]
        re[t] = lin(zip(ce, (e01, e10, p, q)))
        im[t] = lin(zip(co, (o01, o10, po, qo)))
    for t in (1, 2, 3):
        ce, co = TABLE[0, t], TABLE[1, t]
        a, b = lin(zip(ce[:3], (e01, e10, p))), lin([(ce[3], q)])
        re[t], re[8 - t] = a + b, a - b
        a = lin([(co[0], o01), (co[3], qo)])
        b = lin([(co[1], o10), (co[2], po)])
        im[t], im[8 - t] = a + b, a - b
    return re, im


def tile_kernel(dust, flags, to_far, to_near, tile, pack, bits, sems):
    tile_copy = pltpu.make_async_copy(dust, tile, sems.at[0])
    flag_copy = pltpu.make_async_copy(flags, bits, sems.at[1])
    tile_copy.start()
    flag_copy.start()
    lane = lax.broadcasted_iota(jnp.int32, (8, 128), 1)
    row = jnp.zeros((8, 128), jnp.float32)
    flag_copy.wait()
    for i in range(4):
        row = jnp.where(lane == FLAG_LANE + i, bits[0, 0, i].astype(jnp.float32), row)
    tile_copy.wait()
    edges = jnp.where(lane < 64, tile[:, 0:128], tile[:, 896:1024])
    edges = jnp.where((lane < 16) | (lane >= 112), edges, row)
    pack[...] = edges
    to_near[48:56] = edges
    to_far[48:56] = edges
    odd = lax.axis_index("core") == 1
    for b in range(8):
        first, last = tile[0:6, blk(b)], tile[2:8, blk(b)]
        to_near[pl.ds(b, 6, stride=8), :] = jnp.where(odd, first, last)
        to_far[pl.ds(b, 6, stride=8), :] = jnp.where(odd, last, first)


def weight_kernel(bw, wx):
    grow = lax.broadcasted_iota(jnp.int32, (128, 1024), 1) // 8 == lax.broadcasted_iota(
        jnp.int32, (128, 1024), 0
    )
    wide = jnp.dot(
        bw[...].astype(jnp.bfloat16),
        grow.astype(jnp.bfloat16),
        preferred_element_type=jnp.float32,
    )
    for b in range(8):
        wx[b] = wide[:, blk(b)]


def sorted_pair(near, far, odd):
    return jnp.where(odd, near, far), jnp.where(odd, far, near)


def pack_kernel(pack, near, far, _, out):
    out[:, 0:128] = pack[...]
    a, b = sorted_pair(near[48:56], far[48:56], lax.axis_index("core") == 1)
    out[:, 128:256] = a
    out[:, 256:384] = b


def blk(b):
    return slice(128 * b, 128 * b + 128)


def lanes():
    return lax.broadcasted_iota(jnp.int32, (8, 128), 1)


def rows_of():
    return lax.broadcasted_iota(jnp.int32, (8, 128), 0)


def revl(v):
    return jnp.take_along_axis(v, 127 - lanes(), axis=1, mode="promise_in_bounds")


def revr(v):
    return jnp.take_along_axis(v, 7 - rows_of(), axis=0, mode="promise_in_bounds")


def flag(pack, i):
    return jnp.broadcast_to(pack[:, FLAG_LANE + i : FLAG_LANE + i + 1], (8, 128)) > 0.5


def spread(ref, *at):
    *lead, r = at
    return ref[(*lead, pl.ds(r, 8, stride=0), slice(None))]


def place_tiles(own, near_f, far_f, packs, xt, xud, blocks):
    odd_f = lax.axis_index("core") == 1
    pt, pu, pd = (packs[:, blk(i)] for i in range(3))
    f0, f1, f0d, f1u = flag(pt, 0), flag(pt, 1), flag(pd, 0), flag(pu, 1)

    def six_rows(b):
        rows = pl.ds(b, 6, stride=8)
        return sorted_pair(near_f[rows, :], far_f[rows, :], odd_f)

    def pad(v):
        return jnp.concatenate([v, v[0:2]], 0)

    for b in blocks:
        b, c = b - 1, 8 - b
        t_b, t_r = own[:, blk(b)], revl(own[:, blk(c)])
        u_b, d_b = six_rows(b)
        u_r, d_r = six_rows(c)
        xt[4:12, blk(b + 1)] = t_b
        xt[0:4, blk(b + 1)] = jnp.where(f0, revl(pad(u_r)), pad(u_b))[2:6]
        xt[12:16, blk(b + 1)] = jnp.where(f1, revl(pad(d_r)), pad(d_b))[0:4]
        xud[0:6, blk(b + 1)] = u_b
        xud[6:8, blk(b + 1)] = jnp.where(f1u, t_r, t_b)[0:2]
        xud[8:10, blk(b + 1)] = jnp.where(f0d, t_r, t_b)[6:8]
        xud[10:16, blk(b + 1)] = d_b


def place_rims(packs, near_p, far_p, xt, xud):
    low = lanes() < 64
    odd_p = lax.axis_index("y") % 2 == 1
    pt, pu, pd = (packs[:, blk(i)] for i in range(3))
    (plf, prt), (pul, pur), (pdl, pdr) = (
        sorted_pair(near_p[:, blk(i)], far_p[:, blk(i)], odd_p) for i in range(3)
    )
    w_ = jnp.where
    turn_t, turn_u, turn_d = revr(pt), revr(pu), revr(pd)
    revl_l, revl_r = revl(plf), revl(prt)
    xt[4:12, blk(0)] = w_(flag(pt, 2), revr(plf), plf)
    xt[0:4, blk(0)] = pul[4:8]
    xt[12:16, blk(0)] = pdl[0:4]
    xt[4:12, blk(9)] = w_(flag(pt, 3), revr(prt), prt)
    xt[0:4, blk(9)] = pur[4:8]
    xt[12:16, blk(9)] = pdr[0:4]
    xud[0:6, blk(0)] = w_(flag(pu, 2), revr(pul), pul)[2:8]
    xud[6:8, blk(0)] = plf[0:2]
    xud[8:10, blk(0)] = plf[6:8]
    xud[10:16, blk(0)] = w_(flag(pd, 2), revr(pdl), pdl)[0:6]
    xud[0:6, blk(9)] = w_(flag(pu, 3), revr(pur), pur)[2:8]
    xud[6:8, blk(9)] = prt[0:2]
    xud[8:10, blk(9)] = prt[6:8]
    xud[10:16, blk(9)] = w_(flag(pd, 3), revr(pdr), pdr)[0:6]
    xt[4:12, blk(10)] = w_(low, w_(flag(plf, 3), turn_t, pt), plf)
    xt[0:4, blk(10)] = w_(low, pu, w_(flag(plf, 0), revl(pul), pul))[4:8]
    xt[12:16, blk(10)] = w_(low, pd, w_(flag(plf, 1), revl(pdl), pdl))[0:4]
    xt[4:12, blk(11)] = w_(low, prt, w_(flag(prt, 2), turn_t, pt))
    xt[0:4, blk(11)] = w_(low, w_(flag(prt, 0), revl(pur), pur), pu)[4:8]
    xt[12:16, blk(11)] = w_(low, w_(flag(prt, 1), revl(pdr), pdr), pd)[0:4]
    xud[0:6, blk(10)] = w_(low, w_(flag(pul, 3), turn_u, pu), pul)[2:8]
    xud[6:8, blk(10)] = w_(low, pt, w_(flag(pul, 1), revl_l, plf))[0:2]
    xud[8:10, blk(10)] = w_(low, pt, w_(flag(pdl, 0), revl_l, plf))[6:8]
    xud[10:16, blk(10)] = w_(low, w_(flag(pdl, 3), turn_d, pd), pdl)[0:6]
    xud[0:6, blk(11)] = w_(low, pur, w_(flag(pur, 2), turn_u, pu))[2:8]
    xud[6:8, blk(11)] = w_(low, w_(flag(pur, 1), revl_r, prt), pt)[0:2]
    xud[8:10, blk(11)] = w_(low, w_(flag(pdr, 0), revl_r, prt), pt)[6:8]
    xud[10:16, blk(11)] = w_(low, pdr, w_(flag(pdr, 2), turn_d, pd))[0:6]


def dust_features(main, rims, fe, mains, sides):
    def load_own(s, b):
        xt, _ = main if 1 <= b <= 8 else rims
        return xt[4 + s : 12 + s, blk(b)]

    def load_ud(s, b):
        _, xud = main if 1 <= b <= 8 else rims
        return jnp.concatenate([xud[2 + s : 6 + s, blk(b)], xud[10 + s : 14 + s, blk(b)]], 0)

    for slot, load, d in ((0, load_own, 1), (1, load_own, 2), (2, load_own, 4), (3, load_ud, 1), (4, load_ud, 2)):
        left, right = shifts(d)
        for b in mains:
            rows = [tuple(load(s, c) for c in (b - 1, b, b + 1)) for s in (-d, 0, d)]
            for k, v in enumerate(features(*rows, left, right)):
                fe[slot, k, b] = v
        if d == 4:
            continue
        for b, dst in sides:
            rows = [load(s, b) for s in (-d, 0, d)]
            turn_l, turn_r = (lambda v: pltpu.roll(v, d, 1)), (lambda v: pltpu.roll(v, 128 - d, 1))
            for k, v in enumerate(features(*rows, turn_l, turn_r)):
                fe[slot, k, dst] = v


def shifts(d):
    lane = lanes()
    first, last = lane < d, lane >= 128 - d

    def left(v):
        return pltpu.roll(jnp.where(last, v[0], v[1]), d, 1)

    def right(v):
        return pltpu.roll(jnp.where(first, v[2], v[1]), 128 - d, 1)

    return left, right


def first_layer(fe, wx, blocks, sides, put_m, put_side, put_z, flips, start):
    sub = rows_of()

    def column(vals):
        out = jnp.full((8, 128), float(vals[0]), jnp.float32)
        for t in range(1, 8):
            out = jnp.where(sub == t, float(vals[t]), out)
        return out

    ce = [column(TABLE[0, :, k]) for k in range(4)]
    co = [column(TABLE[1, :, k]) for k in range(4)]

    def response(slot, r, b):
        v = [spread(fe, slot, k, b, r) for k in range(8)]
        re = ce[0] * v[0] + ce[1] * v[1] + (ce[2] * v[2] + ce[3] * v[3])
        im = co[0] * v[4] + co[1] * v[5] + (co[2] * v[6] + co[3] * v[7])
        return re, im, re * re + im * im

    powers = []
    for j in range(3):

        def row(r, total, j=j):
            for b in blocks:
                wr = spread(wx, b - 1, r)
                re, im, sq = response(j, r, b)
                total = total + wr * sq
                if j > 0:
                    put_z(j, r, b, wr * re, wr * im)
                if j < 2:
                    put_m(j, 4 + r, b, jnp.sqrt(sq + EPS))
            if j < 2:
                for b in sides:
                    put_side(j, r, b, jnp.sqrt(response(j, r, b)[2] + EPS))
            return total

        powers.append(lax.fori_loop(0, 8, row, start[j]))
    for j in range(2):

        def rim_row(i, _, j=j):
            for r, dst, f in ((i, i, flips[0]), (i + 4, i + 12, flips[1])):
                m = {b: jnp.sqrt(response(3 + j, r, b)[2] + EPS) for b in (*blocks, *sides)}
                for b in blocks:
                    put_m(j, dst, b, jnp.where(f, revl(m[9 - b]), m[b]))
                for b in sides:
                    put_m(j, dst, b, m[b])
            return 0

        lax.fori_loop(0, 4, rim_row, 0)
    return powers


def second_layer(q, blocks, get_m, get_z, wx, put_energy, start):
    j1, j2 = PAIRS[q]
    d = 2**j2
    left, right = shifts(d)

    def row(r, carry):
        carry = list(carry)
        for b in blocks:
            rows = [tuple(get_m(j1, r + (4 + s), c) for c in (b - 1, b, b + 1)) for s in (-d, 0, d)]
            re, im = combos(features(*rows, left, right))
            wr = spread(wx, b - 1, r)
            energy = None
            for t in range(8):
                carry[t] = carry[t] + (get_z(j2, 0, r, b, t) * re[t] + get_z(j2, 1, r, b, t) * im[t])
                sq = re[t] * re[t] + im[t] * im[t]
                carry[8 + t] = carry[8 + t] + wr * sq
                energy = sq if energy is None else energy + sq
            put_energy(q, r, b, energy)
        return tuple(carry)

    return lax.fori_loop(0, 8, row, tuple(start))


INNER = (2, 3, 4, 5, 6, 7)
OUTER = (1, 8)
CORE = (3, 4, 5, 6)
EDGE = {0: 0, 1: 1, 8: 2, 9: 3}


def inner_kernel(own, near_f, far_f, packs, wx, mm, zz, xt, xud, powers, sums, energies, fe):
    f32 = jnp.float32
    place_tiles(own, near_f, far_f, packs, xt, xud, range(1, 9))
    dust_features((xt, xud), None, fe, INNER, ())

    def put_m(j, r, b, v):
        mm[j, r, b - 2] = v

    def put_z(j, r, b, re, im):
        zz[j - 1, 0, r, b - 2] = re
        zz[j - 1, 1, r, b - 2] = im

    pt = packs[:, blk(0)]
    zero = jnp.zeros((8, 128), f32)
    out = first_layer(
        fe, wx, INNER, (), put_m, None, put_z, (flag(pt, 0), flag(pt, 1)), [zero] * 3
    )
    for j in range(3):
        powers[j] = out[j]

    def put_energy(q, r, b, v):
        energies[r, b - 3] = v

    out = second_layer(
        0,
        CORE,
        lambda j, r, b: mm[j, r, b - 2],
        lambda j, ri, r, b, t: spread(zz, j - 1, ri, r, b - 2, t),
        wx,
        put_energy,
        [zero] * 16,
    )
    for k in range(16):
        sums[k] = out[k]


def outer_kernel(packs, near_p, far_p, wx, mi, zi, xt, xud, powers, sums, energies, stats, en0, en1, xtr, xudr, fe, mo, zo, sm, es, acc):
    f32 = jnp.float32
    place_rims(packs, near_p, far_p, xtr, xudr)
    dust_features((xt, xud), (xtr, xudr), fe, OUTER, ((10, 0), (11, 9)))

    def put_m(j, r, b, v):
        mo[j, r, EDGE[b]] = v

    def put_side(j, r, b, v):
        sm[j, b // 9, r] = v

    def put_z(j, r, b, re, im):
        zo[j - 1, 0, r, b // 8] = re
        zo[j - 1, 1, r, b // 8] = im

    pt = packs[:, blk(0)]
    f2, f3 = flag(pt, 2), flag(pt, 3)
    power = first_layer(
        fe,
        wx,
        OUTER,
        (0, 9),
        put_m,
        put_side,
        put_z,
        (flag(pt, 0), flag(pt, 1)),
        [powers[j] for j in range(3)],
    )
    for j in range(2):
        for r in range(8):
            mo[j, 4 + r, EDGE[0]] = jnp.where(f2, sm[j, 0, 7 - r], sm[j, 0, r])
            mo[j, 4 + r, EDGE[9]] = jnp.where(f3, sm[j, 1, 7 - r], sm[j, 1, r])

    def get_m(j, r, b):
        return mo[j, r, EDGE[b]] if b in EDGE else mi[j, r, b - 2]

    def get_z(j, ri, r, b, t):
        if b in EDGE:
            return spread(zo, j - 1, ri, r, b // 8, t)
        return spread(zi, j - 1, ri, r, b - 2, t)

    def put_energy(q, r, b, v):
        if q == 1:
            v = v + (energies[r, b - 3] if b in CORE else es[0, r, :, blk(b - 1)])
        es[q // 2, r, :, blk(b - 1)] = v

    zero = jnp.zeros((8, 128), f32)
    for q in range(3):
        blocks = (1, 2, 7, 8) if q == 0 else range(1, 9)
        start = [sums[k] for k in range(16)] if q == 0 else [zero] * 16
        out = second_layer(q, blocks, get_m, get_z, wx, put_energy, start)
        for k in range(16):
            kind, t = divmod(k, 8)
            acc[pl.ds(q * 128 + kind * 64 + t, 8, stride=8), :] = out[k]
    for r in range(8):
        en0[r : r + 1, :] = jnp.sum(es[0, r], axis=0, keepdims=True)
        en1[r : r + 1, :] = jnp.sum(es[1, r], axis=0, keepdims=True)
    lanes_summed = lax.dot_general(
        jnp.ones((8, 128), f32),
        acc[...],
        (((1,), (1,)), ((), ())),
        precision=lax.Precision.HIGHEST,
        preferred_element_type=f32,
    )
    w_sum = wx[0]
    for b in range(1, 8):
        w_sum = w_sum + wx[b]
    tail = jnp.zeros((1, 128), f32)
    for i, v in enumerate(power + [w_sum]):
        tail = jnp.where(lanes()[0:1] == i, jnp.sum(v), tail)
    for c in range(stats.shape[0]):
        for q in range(3):
            stats[c, q : q + 1, :] = lanes_summed[0:1, blk(q)]
        stats[c, 3:4, :] = tail


def middle_kernel(parts, out, *, n_y):
    x = lax.axis_index("x")
    total = parts[0]
    for i in range(1, parts.shape[0]):
        total = total + parts[i]
    mine = parts[x * n_y]
    for i in range(1, n_y):
        mine = mine + parts[x * n_y + i]
    for i in range(out.shape[0]):
        out[i, 0:4] = total
        out[i, 4:8] = mine


def final_kernel(parts, en0, en1, face_out, sky_out, energy, *, n_zl):
    first = (lax.axis_index("zh") * lax.axis_size("core") + lax.axis_index("core")) * n_zl
    total = parts[0, 0:4]
    for i in range(1, parts.shape[0]):
        total = total + parts[i, 0:4]
    mine = parts[first, 4:8]
    for i in range(1, n_zl):
        mine = mine + parts[first + i, 4:8]
    weight = total[3:4, 3:4]
    level = [total[3:4, j : j + 1] / (8.0 * weight) + EPS for j in range(3)]
    scale = [1.0 / jnp.sqrt(v) for v in level]
    lane = lax.broadcasted_iota(jnp.int32, (1, 128), 1)
    for q, (j1, j2) in enumerate(PAIRS):
        third = jnp.broadcast_to(scale[j1] * scale[j2], (1, 128))
        fourth = jnp.broadcast_to(1.0 / level[j1], (1, 128))
        factor = jnp.where(lane < 64, third, fourth)
        sky_out[q : q + 1, :] = total[q : q + 1] * (factor / weight)
        face_out[q, 0:1, :] = mine[q : q + 1] * (factor / mine[3:4, 3:4])
    a = jnp.broadcast_to(1.0 / (192.0 * level[0]), (8, 1024))
    b = jnp.broadcast_to(1.0 / (192.0 * level[1]), (8, 1024))
    energy[...] = en0[...] * a + en1[...] * b


def pair_exchange(to_near, to_far, axes):
    n = lax.axis_size(axes)
    far = lax.ppermute(to_far, axes, [(i, (i + (1 if i % 2 else n - 1)) % n) for i in range(n)])
    near = lax.ppermute(to_near, axes, [(i, i ^ 1) for i in range(n)])
    return near, far


def on_device(dust, seam_flags, block_weights):
    f32 = jnp.float32
    sds = jax.ShapeDtypeStruct
    vmem = pl.BlockSpec(memory_space=pltpu.VMEM)
    hbm = pl.BlockSpec(memory_space=pltpu.HBM)
    to_far, to_near, tile, pack = pl.pallas_call(
        tile_kernel,
        out_shape=(sds((56, 128), f32), sds((56, 128), f32), sds((8, 1024), f32), sds((8, 128), f32)),
        in_specs=[hbm, hbm],
        out_specs=(vmem,) * 4,
        scratch_shapes=[pltpu.SMEM((1, 1, 4), jnp.int32), pltpu.SemaphoreType.DMA((2,))],
        compiler_params=pltpu.CompilerParams(vmem_limit_bytes=2 << 20),
        name="tile_and_flags",
    )(*(pltpu.with_memory_space_constraint(v, pltpu.HBM) for v in (dust, seam_flags)))
    near_f, far_f = pair_exchange(to_near, to_far, FACE)
    weights = pl.pallas_call(
        weight_kernel,
        out_shape=sds((8, 8, 128), f32),
        in_specs=[vmem],
        out_specs=vmem,
        compiler_params=pltpu.CompilerParams(vmem_limit_bytes=2 << 20),
        name="pixel_weights",
    )(block_weights)
    packs = pl.pallas_call(
        pack_kernel,
        out_shape=sds((8, 384), f32),
        in_specs=[vmem] * 4,
        out_specs=vmem,
        compiler_params=pltpu.CompilerParams(vmem_limit_bytes=2 << 20),
        name="edge_packs",
    )(pack, near_f, far_f, weights)
    near_p, far_p = pair_exchange(packs, packs, PATCH)
    inner = pl.pallas_call(
        inner_kernel,
        out_shape=(
            sds((2, 16, 6, 8, 128), f32),
            sds((2, 2, 8, 6, 8, 128), f32),
            sds((16, 1536), f32),
            sds((16, 1536), f32),
            sds((3, 8, 128), f32),
            sds((16, 8, 128), f32),
            sds((8, 4, 8, 128), f32),
        ),
        in_specs=[vmem] * 5,
        out_specs=(vmem,) * 7,
        scratch_shapes=[
            pltpu.VMEM((5, 8, 10, 8, 128), f32),
        ],
        compiler_params=pltpu.CompilerParams(vmem_limit_bytes=14 << 20),
        name="inner_columns",
    )(tile, near_f, far_f, packs, weights)
    n_y, n_zl = lax.axis_size("y"), lax.axis_size("zl")
    n_first, n_second = lax.axis_size(("x", "y")), lax.axis_size(("zh", "core", "zl"))
    stats, en0, en1 = pl.pallas_call(
        outer_kernel,
        out_shape=(sds((n_first, 4, 128), f32), sds((8, 1024), f32), sds((8, 1024), f32)),
        in_specs=[vmem] * 11,
        out_specs=(vmem,) * 3,
        scratch_shapes=[
            pltpu.VMEM((16, 1536), f32),
            pltpu.VMEM((16, 1536), f32),
            pltpu.VMEM((5, 8, 10, 8, 128), f32),
            pltpu.VMEM((2, 16, 4, 8, 128), f32),
            pltpu.VMEM((2, 2, 8, 2, 8, 128), f32),
            pltpu.VMEM((2, 2, 8, 8, 128), f32),
            pltpu.VMEM((2, 8, 8, 1024), f32),
            pltpu.VMEM((384, 128), f32),
        ],
        compiler_params=pltpu.CompilerParams(vmem_limit_bytes=14 << 20),
        name="both_layers",
    )(packs, near_p, far_p, weights, *inner)
    stats = lax.all_to_all(stats, ("x", "y"), 0, 0, tiled=True)
    stats = pl.pallas_call(
        lambda *refs: middle_kernel(*refs, n_y=n_y),
        out_shape=sds((n_second, 8, 128), f32),
        in_specs=[vmem],
        out_specs=vmem,
        compiler_params=pltpu.CompilerParams(vmem_limit_bytes=2 << 20),
        name="row_part",
    )(stats)
    stats = lax.all_to_all(stats, ("zh", "core", "zl"), 0, 0, tiled=True)
    face_moments, sky_moments, energy = pl.pallas_call(
        lambda *refs: final_kernel(*refs, n_zl=n_zl),
        out_shape=(sds((3, 1, 128), f32), sds((3, 128), f32), sds((8, 1024), f32)),
        in_specs=[vmem] * 3,
        out_specs=(vmem,) * 3,
        compiler_params=pltpu.CompilerParams(vmem_limit_bytes=2 << 20),
        name="finish",
    )(stats, en0, en1)
    return energy, jnp.swapaxes(face_moments, 0, 1), sky_moments


def solution(mesh):
    fine = Mesh(mesh.devices.reshape(4, 2, 2, 4, 8), FACE + PATCH)
    return jax.shard_map(
        on_device,
        mesh=fine,
        in_specs=(P(FACE, PATCH), P(FACE, PATCH, None), P(FACE, PATCH)),
        out_specs=(P(FACE, PATCH), P(FACE, None, None), P()),
        check_vma=False,
    )
```

profile of v0, /device:TPU:1, one launch (start us, length us, event | category | flops | bytes accessed | tf_op | source)
XLA Modules:
  0.0 69.2 jit_solution(17551487198583709479)
XLA Ops:
  0.6 0.0 copy-start
  0.6 0.8 %tile_and_flags.1 = (f32[56,128]{1,0:T(8,128)S(1)}, f32[56,128]{1,0:T(8,128)S(1)}, f32[8,1024]{1,0:T(8,128)S(1)}, f32[8,128]{1,0:T(8,128)S(1)}) custom-call(f32[8,1024]{1,0:T(8,128)} %dust.1, s32[1,1,4]{2,1,0:T(1,128)} %flags.1), custom_call_target="tpu_custom_call" | custom-call | tf_op jit(solution)/shard_map/tile_and_flags/pallas_call | solution.py:509
  1.5 8.7 %collective-permute-start = (f32[56,128]{1,0:T(8,128)S(1)}, f32[56,128]{1,0:T(8,128)S(1)}, u32[]{:S(2)}, u32[]{:S(2)}) collective-permute-start(f32[56,128]{1,0:T(8,128)S(1)} %get-tuple-element.21), channel_id=1, source_target_pairs={{0,32},{32,0},{64,96},{96,64},{128,160},{160,128},{192,224},{224,1... | collective-permute-start | bytes 86024 | tf_op jit(solution)/shard_map/ppermute | solution.py:500
  10.2 5.2 %collective-permute-start.1 = (f32[56,128]{1,0:T(8,128)S(1)}, f32[56,128]{1,0:T(8,128)S(1)}, u32[]{:S(2)}, u32[]{:S(2)}) collective-permute-start(f32[56,128]{1,0:T(8,128)S(1)} %get-tuple-element.22), channel_id=1, source_target_pairs={{0,480},{32,64},{64,32},{96,128},{128,96},{160,192},{192,160},{224... | collective-permute-start | bytes 86024 | tf_op jit(solution)/shard_map/ppermute | solution.py:499
  15.4 0.0 copy-done
  15.5 0.1 pixel_weights.1._.wx
  15.6 0.0 collective-permute-done.near.near_f
  15.6 3.7 %collective-permute-done.1.far.far_f = f32[56,128]{1,0:T(8,128)S(1)} collective-permute-done((f32[56,128]{1,0:T(8,128)S(1)}, f32[56,128]{1,0:T(8,128)S(1)}, u32[]{:S(2)}, u32[]{:S(2)}) %collective-permute-start.1) | collective-permute-done | bytes 28704 | tf_op jit(solution)/shard_map/ppermute | solution.py:499
  19.3 5.7 %collective-permute-start.3 = (f32[8,384]{1,0:T(8,128)S(1)}, f32[8,384]{1,0:T(8,128)S(1)}, u32[]{:S(2)}, u32[]{:S(2)}) collective-permute-start(f32[8,384]{1,0:T(8,128)S(1)} %edge_packs.1.packs), channel_id=1, source_target_pairs={{0,31},{1,2},{2,1},{3,4},{4,3},{5,6},{6,5},{7,8},{8,7},{9,10},{10,... | collective-permute-start | bytes 36872 | tf_op jit(solution)/shard_map/ppermute | solution.py:499
  25.1 1.9 %collective-permute-start.2 = (f32[8,384]{1,0:T(8,128)S(1)}, f32[8,384]{1,0:T(8,128)S(1)}, u32[]{:S(2)}, u32[]{:S(2)}) collective-permute-start(f32[8,384]{1,0:T(8,128)S(1)} %edge_packs.1.packs), channel_id=1, source_target_pairs={{0,1},{1,0},{2,3},{3,2},{4,5},{5,4},{6,7},{7,6},{8,9},{9,8},{10,11... | collective-permute-start | bytes 36872 | tf_op jit(solution)/shard_map/ppermute | solution.py:500
  27.0 3.4 %inner_columns.1 = (f32[2,16,6,8,128]{4,3,2,1,0:T(8,128)S(1)}, f32[2,2,8,6,8,128]{5,4,3,2,1,0:T(8,128)S(1)}, f32[16,1536]{1,0:T(8,128)S(1)}, f32[16,1536]{1,0:T(...) custom-call(f32[8,1024]{1,0:T(8,128)S(1)} %get-tuple-element.23.own, ...), custom_call_target="tpu_custom_call" | custom-call | tf_op jit(solution)/shard_map/inner_columns/pallas_call | solution.py:536
  30.4 0.0 collective-permute-done.3.far_p
  30.4 0.0 collective-permute-done.2.near_p
  30.4 7.1 %both_layers.1 = (f32[32,4,128]{2,1,0:T(4,128)S(1)}, f32[8,1024]{1,0:T(8,128)S(1)}, f32[8,1024]{1,0:T(8,128)S(1)}) custom-call(f32[8,384]{1,0:T(8,128)S(1)} %edge_packs.1.packs, f32[8,384]{1,0:T(8,128)S(1)} %collective-permute-done.2.near_p, f32[8,384]{1,0:T(8,128)S(1)} %collective-permute-done.3.far_p, f32[8,8,128]{2,1,0:T(8,128)S(1)} %pixel_weights.1._.wx, ...), custom_call_target="tpu_custom_call" | custom-call | tf_op jit(solution)/shard_map/both_layers/pallas_call | solution.py:557
  37.5 14.4 %all_to_all.10.refs_0_ = f32[32,4,128]{2,1,0:T(4,128)S(1)} all-to-all(f32[32,4,128]{2,1,0:T(4,128)S(1)} %get-tuple-element.31), channel_id=1, replica_groups=mesh['x'=4,'zh'=2,'core'=2,'zl'=4,'y'=8] {'x','y'}, dimensions={0} | all-to-all | bytes 131072 | tf_op jit(solution)/shard_map/all_to_all | solution.py:575
  51.9 16.4 %all_to_all.11.refs_0_ = f32[16,8,128]{2,1,0:T(8,128)S(1)} all-to-all(f32[16,8,128]{2,1,0:T(8,128)S(1)} %row_part.1), channel_id=1, replica_groups=mesh['x'=4,'zh'=2,'core'=2,'zl'=4,'y'=8] {'zh','core','zl'}, dimensions={0} | all-to-all | bytes 131072 | tf_op jit(solution)/shard_map/all_to_all | solution.py:584
  68.4 0.9 %finish.1 = (f32[3,1,128]{2,1,0:T(1,128)}, f32[3,128]{1,0:T(4,128)}, f32[8,1024]{1,0:T(8,128)}) custom-call(f32[16,8,128]{2,1,0:T(8,128)S(1)} %all_to_all.11.refs_0_, f32[8,1024]{1,0:T(8,128)S(1)} %get-tuple-element.32.refs_1_, f32[8,1024]{1,0:T(8,128)S(1)} %get-tuple-element.33.refs_2_), custom_call_target="tpu_custom_call" | custom-call | tf_op jit(solution)/shard_map/finish/pallas_call | solution.py:585
  (2 shorter events, 0.0 us)
Async XLA Ops:
  0.6 14.8 %copy-start = (s32[8,128]{1,0:T(8,128)S(1)}, s32[8,128]{1,0:T(8,128)}, u32[]{:S(2)}) copy-start(s32[8,128]{1,0:T(8,128)} %bw.1) | copy-start | bytes 12292
  1.5 14.1 %collective-permute-start = (f32[56,128]{1,0:T(8,128)S(1)}, f32[56,128]{1,0:T(8,128)S(1)}, u32[]{:S(2)}, u32[]{:S(2)}) collective-permute-start(f32[56,128]{1,0:T(8,128)S(1)} %get-tuple-element.21), channel_id=1, source_target_pairs={{0,32},{32,0},{64,96},{96,64},{128,160},{160,128},{192,224},{224,1... | collective-permute-start | bytes 86024 | tf_op jit(solution)/shard_map/ppermute | solution.py:500
  10.2 9.1 %collective-permute-start.1 = (f32[56,128]{1,0:T(8,128)S(1)}, f32[56,128]{1,0:T(8,128)S(1)}, u32[]{:S(2)}, u32[]{:S(2)}) collective-permute-start(f32[56,128]{1,0:T(8,128)S(1)} %get-tuple-element.22), channel_id=1, source_target_pairs={{0,480},{32,64},{64,32},{96,128},{128,96},{160,192},{192,160},{224... | collective-permute-start | bytes 86024 | tf_op jit(solution)/shard_map/ppermute | solution.py:499
  19.3 11.0 %collective-permute-start.3 = (f32[8,384]{1,0:T(8,128)S(1)}, f32[8,384]{1,0:T(8,128)S(1)}, u32[]{:S(2)}, u32[]{:S(2)}) collective-permute-start(f32[8,384]{1,0:T(8,128)S(1)} %edge_packs.1.packs), channel_id=1, source_target_pairs={{0,31},{1,2},{2,1},{3,4},{4,3},{5,6},{6,5},{7,8},{8,7},{9,10},{10,... | collective-permute-start | bytes 36872 | tf_op jit(solution)/shard_map/ppermute | solution.py:499
  25.1 5.3 %collective-permute-start.2 = (f32[8,384]{1,0:T(8,128)S(1)}, f32[8,384]{1,0:T(8,128)S(1)}, u32[]{:S(2)}, u32[]{:S(2)}) collective-permute-start(f32[8,384]{1,0:T(8,128)S(1)} %edge_packs.1.packs), channel_id=1, source_target_pairs={{0,1},{1,0},{2,3},{3,2},{4,5},{5,4},{6,7},{7,6},{8,9},{9,8},{10,11... | collective-permute-start | bytes 36872 | tf_op jit(solution)/shard_map/ppermute | solution.py:500
where the time goes:
time: 69.6 us; the launch traced here: 69.2 us
  blocking collectives  30.8 us (44%)
  starting transfers between devices  21.6 us (31%)
  Pallas kernels  12.4 us (18%)
  waiting for transfers between devices  3.75 us (5%)
  between operations  0.72 us (1%)
    all_to_all x1, blocking collectives, on_device(): stats = lax.all_to_all(stats, ('zh', 'core', 'zl'), 0, 0, tiled=True)  16.4 us
    all_to_all x1, blocking collectives, on_device(): stats = lax.all_to_all(stats, ('x', 'y'), 0, 0, tiled=True)  14.4 us
    ppermute x2, starting transfers between devices, pair_exchange(): lax.ppermute(to_far, axes, [(i, (i + (1 if i % 2 else n - 1)) % n) for i...  10.9 us
    ppermute x2, starting transfers between devices, pair_exchange(): near = lax.ppermute(to_near, axes, [(i, i ^ 1) for i in range(n)])  10.7 us
    pallas_call x1, Pallas kernels, on_device(): pl.pallas_call(outer_kernel, out_shape=(sds((n_first, 4, 128), f32), sds(...  7.13 us
    ppermute x2, waiting for transfers between devices, pair_exchange(): lax.ppermute(to_far, axes, [(i, (i + (1 if i % 2 else n - 1)) % n) for i...  3.75 us
    pallas_call x1, Pallas kernels, on_device(): pl.pallas_call(inner_kernel, out_shape=(sds((2, 16, 6, 8, 128), f32), sds...  3.35 us
  transfers between devices with their start and end apart: 4, of which 1 were waited for; matrix products, arithmetic and copies ran while one was open for 0% of the time, Pallas kernels for 5%

commit v1 on v0

--- a/solution.py
+++ b/solution.py
@@ -346,6 +346,24 @@
 EDGE = {0: 0, 1: 1, 8: 2, 9: 3}
 
 
+def sublane_sums(rows):
+    sub = rows_of()
+    for step in (4, 2, 1):
+        keep = sub % (2 * step) < step
+        merged = []
+        for u, v in zip(rows[:step], rows[step:]):
+            other = jnp.where(keep, v, u)
+            if step == 4:
+                other = pltpu.roll(other, 4, 0)
+            else:
+                other = jnp.where(
+                    keep, pltpu.roll(other, 8 - step, 0), pltpu.roll(other, step, 0)
+                )
+            merged.append(jnp.where(keep, u, v) + other)
+        rows = merged
+    return rows[0]
+
+
 def inner_kernel(own, near_f, far_f, packs, wx, mm, zz, xt, xud, powers, sums, energies, fe):
     f32 = jnp.float32
     place_tiles(own, near_f, far_f, packs, xt, xud, range(1, 9))
@@ -436,9 +454,9 @@
         for k in range(16):
             kind, t = divmod(k, 8)
             acc[pl.ds(q * 128 + kind * 64 + t, 8, stride=8), :] = out[k]
-    for r in range(8):
-        en0[r : r + 1, :] = jnp.sum(es[0, r], axis=0, keepdims=True)
-        en1[r : r + 1, :] = jnp.sum(es[1, r], axis=0, keepdims=True)
+    for plane, out_ref in ((0, en0), (1, en1)):
+        for b in range(8):
+            out_ref[:, blk(b)] = sublane_sums([es[plane, r, :, blk(b)] for r in range(8)])
     lanes_summed = lax.dot_general(
         jnp.ones((8, 128), f32),
         acc[...],

time: 69.6 us -> 69.5 us (level)
  no operation moved by 1% of the time
where the time goes in v1:
time: 69.5 us; the launch traced here: 69.2 us
  blocking collectives  30.8 us (44%)
  starting transfers between devices  21.6 us (31%)
  Pallas kernels  12.3 us (18%)
  waiting for transfers between devices  3.75 us (5%)
  between operations  0.72 us (1%)
    all_to_all x1, blocking collectives, on_device(): stats = lax.all_to_all(stats, ('zh', 'core', 'zl'), 0, 0, tiled=True)  16.4 us
    all_to_all x1, blocking collectives, on_device(): stats = lax.all_to_all(stats, ('x', 'y'), 0, 0, tiled=True)  14.4 us
    ppermute x2, starting transfers between devices, pair_exchange(): lax.ppermute(to_far, axes, [(i, (i + (1 if i % 2 else n - 1)) % n) for i...  10.9 us
    ppermute x2, starting transfers between devices, pair_exchange(): near = lax.ppermute(to_near, axes, [(i, i ^ 1) for i in range(n)])  10.7 us
    pallas_call x1, Pallas kernels, on_device(): pl.pallas_call(outer_kernel, out_shape=(sds((n_first, 4, 128), f32), sds(...  7.07 us
    ppermute x2, waiting for transfers between devices, pair_exchange(): lax.ppermute(to_far, axes, [(i, (i + (1 if i % 2 else n - 1)) % n) for i...  3.75 us
    pallas_call x1, Pallas kernels, on_device(): pl.pallas_call(inner_kernel, out_shape=(sds((2, 16, 6, 8, 128), f32), sds...  3.35 us
  transfers between devices with their start and end apart: 4, of which 1 were waited for; matrix products, arithmetic and copies ran while one was open for 0% of the time, Pallas kernels for 5%

profile of v1, /device:TPU:1, one launch (start us, length us, event | category | flops | bytes accessed | tf_op | source)
XLA Modules:
  0.0 69.2 jit_solution(10103172001389604500)
XLA Ops:
  0.6 0.0 copy-start
  0.6 0.8 %tile_and_flags.1 = (f32[56,128]{1,0:T(8,128)S(1)}, f32[56,128]{1,0:T(8,128)S(1)}, f32[8,1024]{1,0:T(8,128)S(1)}, f32[8,128]{1,0:T(8,128)S(1)}) custom-call(f32[8,1024]{1,0:T(8,128)} %dust.1, s32[1,1,4]{2,1,0:T(1,128)} %flags.1), custom_call_target="tpu_custom_call" | custom-call | tf_op jit(solution)/shard_map/tile_and_flags/pallas_call | solution.py:527
  1.5 8.7 %collective-permute-start = (f32[56,128]{1,0:T(8,128)S(1)}, f32[56,128]{1,0:T(8,128)S(1)}, u32[]{:S(2)}, u32[]{:S(2)}) collective-permute-start(f32[56,128]{1,0:T(8,128)S(1)} %get-tuple-element.21), channel_id=1, source_target_pairs={{0,32},{32,0},{64,96},{96,64},{128,160},{160,128},{192,224},{224,1... | collective-permute-start | bytes 86024 | tf_op jit(solution)/shard_map/ppermute | solution.py:518
  10.2 5.2 %collective-permute-start.1 = (f32[56,128]{1,0:T(8,128)S(1)}, f32[56,128]{1,0:T(8,128)S(1)}, u32[]{:S(2)}, u32[]{:S(2)}) collective-permute-start(f32[56,128]{1,0:T(8,128)S(1)} %get-tuple-element.22), channel_id=1, source_target_pairs={{0,480},{32,64},{64,32},{96,128},{128,96},{160,192},{192,160},{224... | collective-permute-start | bytes 86024 | tf_op jit(solution)/shard_map/ppermute | solution.py:517
  15.4 0.0 copy-done
  15.5 0.1 pixel_weights.1._.wx
  15.6 0.0 collective-permute-done.near.near_f
  15.6 3.7 %collective-permute-done.1.far.far_f = f32[56,128]{1,0:T(8,128)S(1)} collective-permute-done((f32[56,128]{1,0:T(8,128)S(1)}, f32[56,128]{1,0:T(8,128)S(1)}, u32[]{:S(2)}, u32[]{:S(2)}) %collective-permute-start.1) | collective-permute-done | bytes 28704 | tf_op jit(solution)/shard_map/ppermute | solution.py:517
  19.3 5.7 %collective-permute-start.3 = (f32[8,384]{1,0:T(8,128)S(1)}, f32[8,384]{1,0:T(8,128)S(1)}, u32[]{:S(2)}, u32[]{:S(2)}) collective-permute-start(f32[8,384]{1,0:T(8,128)S(1)} %edge_packs.1.packs), channel_id=1, source_target_pairs={{0,31},{1,2},{2,1},{3,4},{4,3},{5,6},{6,5},{7,8},{8,7},{9,10},{10,... | collective-permute-start | bytes 36872 | tf_op jit(solution)/shard_map/ppermute | solution.py:517
  25.1 1.9 %collective-permute-start.2 = (f32[8,384]{1,0:T(8,128)S(1)}, f32[8,384]{1,0:T(8,128)S(1)}, u32[]{:S(2)}, u32[]{:S(2)}) collective-permute-start(f32[8,384]{1,0:T(8,128)S(1)} %edge_packs.1.packs), channel_id=1, source_target_pairs={{0,1},{1,0},{2,3},{3,2},{4,5},{5,4},{6,7},{7,6},{8,9},{9,8},{10,11... | collective-permute-start | bytes 36872 | tf_op jit(solution)/shard_map/ppermute | solution.py:518
  27.0 3.4 %inner_columns.1 = (f32[2,16,6,8,128]{4,3,2,1,0:T(8,128)S(1)}, f32[2,2,8,6,8,128]{5,4,3,2,1,0:T(8,128)S(1)}, f32[16,1536]{1,0:T(8,128)S(1)}, f32[16,1536]{1,0:T(...) custom-call(f32[8,1024]{1,0:T(8,128)S(1)} %get-tuple-element.23.own, ...), custom_call_target="tpu_custom_call" | custom-call | tf_op jit(solution)/shard_map/inner_columns/pallas_call | solution.py:554
  30.4 0.0 collective-permute-done.3.far_p
  30.4 0.0 collective-permute-done.2.near_p
  30.4 7.1 %both_layers.1 = (f32[32,4,128]{2,1,0:T(4,128)S(1)}, f32[8,1024]{1,0:T(8,128)S(1)}, f32[8,1024]{1,0:T(8,128)S(1)}) custom-call(f32[8,384]{1,0:T(8,128)S(1)} %edge_packs.1.packs, f32[8,384]{1,0:T(8,128)S(1)} %collective-permute-done.2.near_p, f32[8,384]{1,0:T(8,128)S(1)} %collective-permute-done.3.far_p, f32[8,8,128]{2,1,0:T(8,128)S(1)} %pixel_weights.1._.wx, ...), custom_call_target="tpu_custom_call" | custom-call | tf_op jit(solution)/shard_map/both_layers/pallas_call | solution.py:575
  37.5 14.4 %all_to_all.10.refs_0_ = f32[32,4,128]{2,1,0:T(4,128)S(1)} all-to-all(f32[32,4,128]{2,1,0:T(4,128)S(1)} %get-tuple-element.31), channel_id=1, replica_groups=mesh['x'=4,'zh'=2,'core'=2,'zl'=4,'y'=8] {'x','y'}, dimensions={0} | all-to-all | bytes 131072 | tf_op jit(solution)/shard_map/all_to_all | solution.py:593
  51.9 16.4 %all_to_all.11.refs_0_ = f32[16,8,128]{2,1,0:T(8,128)S(1)} all-to-all(f32[16,8,128]{2,1,0:T(8,128)S(1)} %row_part.1), channel_id=1, replica_groups=mesh['x'=4,'zh'=2,'core'=2,'zl'=4,'y'=8] {'zh','core','zl'}, dimensions={0} | all-to-all | bytes 131072 | tf_op jit(solution)/shard_map/all_to_all | solution.py:602
  68.3 0.9 %finish.1 = (f32[3,1,128]{2,1,0:T(1,128)}, f32[3,128]{1,0:T(4,128)}, f32[8,1024]{1,0:T(8,128)}) custom-call(f32[16,8,128]{2,1,0:T(8,128)S(1)} %all_to_all.11.refs_0_, f32[8,1024]{1,0:T(8,128)S(1)} %get-tuple-element.32.refs_1_, f32[8,1024]{1,0:T(8,128)S(1)} %get-tuple-element.33.refs_2_), custom_call_target="tpu_custom_call" | custom-call | tf_op jit(solution)/shard_map/finish/pallas_call | solution.py:603
  (2 shorter events, 0.0 us)
Async XLA Ops:
  0.6 14.8 %copy-start = (s32[8,128]{1,0:T(8,128)S(1)}, s32[8,128]{1,0:T(8,128)}, u32[]{:S(2)}) copy-start(s32[8,128]{1,0:T(8,128)} %bw.1) | copy-start | bytes 12292
  1.5 14.1 %collective-permute-start = (f32[56,128]{1,0:T(8,128)S(1)}, f32[56,128]{1,0:T(8,128)S(1)}, u32[]{:S(2)}, u32[]{:S(2)}) collective-permute-start(f32[56,128]{1,0:T(8,128)S(1)} %get-tuple-element.21), channel_id=1, source_target_pairs={{0,32},{32,0},{64,96},{96,64},{128,160},{160,128},{192,224},{224,1... | collective-permute-start | bytes 86024 | tf_op jit(solution)/shard_map/ppermute | solution.py:518
  10.2 9.1 %collective-permute-start.1 = (f32[56,128]{1,0:T(8,128)S(1)}, f32[56,128]{1,0:T(8,128)S(1)}, u32[]{:S(2)}, u32[]{:S(2)}) collective-permute-start(f32[56,128]{1,0:T(8,128)S(1)} %get-tuple-element.22), channel_id=1, source_target_pairs={{0,480},{32,64},{64,32},{96,128},{128,96},{160,192},{192,160},{224... | collective-permute-start | bytes 86024 | tf_op jit(solution)/shard_map/ppermute | solution.py:517
  19.3 11.0 %collective-permute-start.3 = (f32[8,384]{1,0:T(8,128)S(1)}, f32[8,384]{1,0:T(8,128)S(1)}, u32[]{:S(2)}, u32[]{:S(2)}) collective-permute-start(f32[8,384]{1,0:T(8,128)S(1)} %edge_packs.1.packs), channel_id=1, source_target_pairs={{0,31},{1,2},{2,1},{3,4},{4,3},{5,6},{6,5},{7,8},{8,7},{9,10},{10,... | collective-permute-start | bytes 36872 | tf_op jit(solution)/shard_map/ppermute | solution.py:517
  25.1 5.3 %collective-permute-start.2 = (f32[8,384]{1,0:T(8,128)S(1)}, f32[8,384]{1,0:T(8,128)S(1)}, u32[]{:S(2)}, u32[]{:S(2)}) collective-permute-start(f32[8,384]{1,0:T(8,128)S(1)} %edge_packs.1.packs), channel_id=1, source_target_pairs={{0,1},{1,0},{2,3},{3,2},{4,5},{5,4},{6,7},{7,6},{8,9},{9,8},{10,11... | collective-permute-start | bytes 36872 | tf_op jit(solution)/shard_map/ppermute | solution.py:518
